TPU v7x, 32 devices: a whole 2x2x4 slice. The times are simulated.
32 devices in a mesh: group: 2 (over x), col: 16 (over z, y, core).
Axes of the slice: x: 2, y: 2, z: 4, core: 2. Of those that a mesh axis runs over, the one named last changes fastest.
Arguments:
- homolog_embedding: bfloat16 [192, 64, 256], P('group', 'col'), parts along dimension 0, may hold values from -6 to 6
- left_factor_matrix: bfloat16 [256, 32], replicated, may hold values from -0.375 to 0.375
- right_factor_matrix: bfloat16 [256, 32], replicated, may hold values from -0.375 to 0.375
- decoder: bfloat16 [1024, 128], replicated, may hold values from -2 to 2
- pair_output_bias: float32 [128], replicated, may hold values from -3 to 3
- pair_output_gradient: bfloat16 [128, 64, 128], P('group', 'col'), parts along dimension 0, may hold values from -6 to 6
Outputs:
- first_operand_gradient: float32 [192, 64, 32], P('group', 'col'), parts along dimension 0
- second_operand_gradient: float32 [192, 64, 32], P('group', 'col'), parts along dimension 0
- alignment_gradient: bfloat16 [192, 64, 256], P('group', 'col'), parts along dimension 0
There are 2 independent parts, one for each index of `group`. A program takes and returns all parts, laid end to end along the dimension named above; an argument that names none is the same for every part. Nothing has to cross between parts.
All inputs are finite; a program needn't handle non-finite values.
Results may differ from a plain program's by a relative error of at most 0.0083.
Values may be sent and summed in bfloat16 or wider, within the bound.
A program may use at most 64 MiB of HBM per device.

v0:
```python
import jax
import jax.numpy as jnp
from jax import lax
from jax.sharding import PartitionSpec as P


def per_device(
    homolog_embedding,
    left_factor_matrix,
    right_factor_matrix,
    decoder,
    pair_output_bias,
    pair_output_gradient,
):
    alignment_row_count, local_residue_start, alignment_channel_width = homolog_embedding.shape
    operand_channel_width = left_factor_matrix.shape[1]
    channels = decoder.shape[1]
    residue_total_count = local_residue_start * lax.axis_size("col")
    reciprocal_rows = 1.0 / alignment_row_count
    block_res = local_residue_start * max(1, 96 // local_residue_start)
    alignment_flattened_rows = homolog_embedding.reshape(
        alignment_row_count * local_residue_start, alignment_channel_width
    )
    first_operand_rows = (
        jnp.dot(alignment_flattened_rows, left_factor_matrix, preferred_element_type=jnp.float32)
        .astype(jnp.bfloat16)
        .reshape(alignment_row_count, local_residue_start * operand_channel_width)
    )
    second_operand_rows = (
        jnp.dot(alignment_flattened_rows, right_factor_matrix, preferred_element_type=jnp.float32)
        .astype(jnp.bfloat16)
        .reshape(alignment_row_count, local_residue_start * operand_channel_width)
    )
    second_operand_local = second_operand_rows.reshape(
        alignment_row_count, local_residue_start, operand_channel_width
    )

    def outer_slopes(slope_rows, rows_by_length, col_span):
        backward = (
            jnp.dot(slope_rows, decoder.T, preferred_element_type=jnp.float32) * reciprocal_rows
        )
        return backward.astype(jnp.bfloat16).reshape(
            rows_by_length, col_span, operand_channel_width, operand_channel_width
        )

    offset_col = jnp.int32(0)
    second_operand_gradient = jnp.zeros(
        (alignment_row_count, local_residue_start, operand_channel_width), jnp.float32
    )
    stored = jnp.zeros((residue_total_count, local_residue_start * channels), jnp.bfloat16)
    left_segment = lax.all_gather(first_operand_rows, "col", axis=1, tiled=True)
    right_segment = lax.all_gather(second_operand_rows, "col", axis=1, tiled=True)
    right_whole = right_segment
    piece_res = left_segment.shape[1] // operand_channel_width
    first_res = offset_col // operand_channel_width
    collected = []
    for split_offset in range(0, piece_res, block_res):
        split_rows_by_length = min(block_res, piece_res - split_offset)
        split_left_block = left_segment[
            :,
            split_offset
            * operand_channel_width : (split_offset + split_rows_by_length)
            * operand_channel_width,
        ].reshape(alignment_row_count, split_rows_by_length, operand_channel_width)
        collected.append((split_rows_by_length, split_left_block, first_res + split_offset))
    for rows_by_length, left_block, first_row in collected:
        products = (
            jnp.einsum(
                "sic,sjd->ijcd",
                left_block,
                second_operand_local,
                preferred_element_type=jnp.float32,
            )
            * reciprocal_rows
        )
        products = products.astype(jnp.bfloat16).reshape(
            rows_by_length * local_residue_start, operand_channel_width * operand_channel_width
        )
        linear = jnp.dot(products, decoder, preferred_element_type=jnp.float32) + pair_output_bias
        upstream = lax.dynamic_slice_in_dim(pair_output_gradient, first_row, rows_by_length, 0)
        upstream = upstream.reshape(rows_by_length * local_residue_start, channels).astype(
            jnp.float32
        )
        accumulate_slope_rows = (upstream * 2.0 * jnp.maximum(linear, 0.0)).astype(jnp.bfloat16)
        stored = lax.dynamic_update_slice_in_dim(
            stored,
            accumulate_slope_rows.reshape(rows_by_length, local_residue_start * channels),
            first_row,
            0,
        )
        accumulate_slopes = outer_slopes(accumulate_slope_rows, rows_by_length, local_residue_start)
        second_operand_gradient = second_operand_gradient + jnp.einsum(
            "ijcd,sic->sjd", accumulate_slopes, left_block, preferred_element_type=jnp.float32
        )
    second_operand_gradient, stored, right_whole = (second_operand_gradient, stored, right_whole)
    received = lax.all_to_all(stored, "col", split_axis=0, concat_axis=1, tiled=True)
    right_all = right_whole.reshape(alignment_row_count, residue_total_count, operand_channel_width)
    col_span = local_residue_start * max(
        max(1, 96 // local_residue_start), lax.axis_size("col") // 8
    )
    first_operand_gradient = jnp.zeros(
        (alignment_row_count, local_residue_start, operand_channel_width), jnp.float32
    )
    for offset in range(0, residue_total_count, col_span):
        width_cols = min(col_span, residue_total_count - offset)
        slope_rows = received[:, offset * channels : (offset + width_cols) * channels].reshape(
            local_residue_start * width_cols, channels
        )
        slopes = outer_slopes(slope_rows, local_residue_start, width_cols)
        first_operand_gradient = first_operand_gradient + jnp.einsum(
            "ijcd,sjd->sic",
            slopes,
            right_all[:, offset : offset + width_cols],
            preferred_element_type=jnp.float32,
        )
    first_operand_gradient_step = first_operand_gradient.astype(jnp.bfloat16).reshape(
        alignment_row_count * local_residue_start, operand_channel_width
    )
    second_operand_gradient_step = second_operand_gradient.astype(jnp.bfloat16).reshape(
        alignment_row_count * local_residue_start, operand_channel_width
    )
    alignment_gradient = jnp.dot(
        first_operand_gradient_step, left_factor_matrix.T, preferred_element_type=jnp.float32
    ) + jnp.dot(
        second_operand_gradient_step, right_factor_matrix.T, preferred_element_type=jnp.float32
    )
    alignment_gradient = alignment_gradient.astype(jnp.bfloat16).reshape(
        alignment_row_count, local_residue_start, alignment_channel_width
    )
    return (first_operand_gradient, second_operand_gradient, alignment_gradient)


def solution(mesh):
    placed = (P("group", "col", None), P(), P(), P(), P(), P("group", "col", None))
    return jax.shard_map(
        per_device,
        mesh=mesh,
        in_specs=placed,
        out_specs=(P("group", "col", None), P("group", "col", None), P("group", "col", None)),
        check_vma=False,
    )
```

profile of v0, /device:TPU:0, one launch (start us, length us, event | category | flops | bytes accessed | tf_op | source)
XLA Modules:
  0.0 74.2 jit_solution(9161705522396213601)
XLA Ops:
  0.7 1.0 %reshape.53 = bf16[384,256]{1,0:T(8,128)(2,1)S(1)} reshape(bf16[96,4,256]{2,1,0:T(4,128)(2,1)} %param.6) | data formatting | bytes 393216 | tf_op jit(solution)/shard_map/reshape | solution.py:21
  1.7 0.9 %convolution_convert_fusion = bf16[384,32]{0,1:T(8,128)(2,1)S(1)} fusion(bf16[384,256]{1,0:T(8,128)(2,1)S(1)} %reshape.53, bf16[256,32]{0,1:T(8,128)(2,1)} %param.7), kind=kOutput, calls=%fused_computation.14 | convolution fusion | flops 6303744 | bytes 237568 | tf_op jit(solution)/shard_map/dot_general | solution.py:25
  2.8 24.2 %all_gather.7 = bf16[96,2048]{1,0:T(8,128)(2,1)S(1)} all-gather(bf16[96,128]{1,0:T(8,128)(2,1)S(1)} %reshape.56), channel_id=1, replica_groups=mesh['group'=2,'col'=16] {'col'}, dimensions={1}, use_global_device_ids=true | all-gather | bytes 417792 | tf_op jit(solution)/shard_map/all_gather | solution.py:51
  27.0 0.3 copy.32
  27.6 1.6 %fusion = bf16[64,4,32,32]{0,3,2,1:T(8,128)(2,1)} fusion(bf16[96,64,32]{0,2,1:T(8,128)(2,1)S(1)} %bitcast.48, bf16[96,4,32,1]{2,1,0,3:T(4,128)(2,1)S(1)} %bitcast.51), kind=kOutput, calls=%fused_computation.1 | convolution fusion | flops 50855936 | bytes 942080 | tf_op jit(solution)/shard_map/sic,sjd->ijcd/dot_general | solution.py:68
  29.3 4.2 %copy.35 = bf16[64,4,32,32]{3,2,1,0:T(8,128)(2,1)S(1)} copy(bf16[64,4,32,32]{0,3,2,1:T(8,128)(2,1)} %fusion) | data formatting | bytes 1048576 | tf_op jit(solution)/shard_map/convert_element_type | solution.py:76
  33.5 2.2 %reshape.58 = bf16[256,1024]{1,0:T(8,128)(2,1)S(1)} reshape(bf16[64,4,32,32]{3,2,1,0:T(8,128)(2,1)S(1)} %copy.35) | data formatting | bytes 1048576 | tf_op jit(solution)/shard_map/reshape | solution.py:76
  35.7 0.9 %convert_multiply_fusion = f32[64,4,128]{2,1,0:T(4,128)S(1)} fusion(bf16[64,4,128]{2,1,0:T(4,128)(2,1)} %param.11), kind=kLoop, calls=%fused_computation.18 | loop fusion | flops 65536 | bytes 196608 | tf_op jit(solution)/shard_map/mul | solution.py:84
  36.6 0.3 fusion.6
  36.9 0.7 all_to_all.12
  37.6 4.2 %all-to-all-start = ((bf16[16,4,512]{2,1,0:T(4,128)(2,1)}), bf16[16,4,512]{2,1,0:T(4,128)(2,1)}, u32[]{:S(2)}, u32[]{:S(2)}) async-start(bf16[16,4,512]{2,1,0:T(4,128)(2,1)} %all_to_all.12), calls=%async_computation | async-start | bytes 131072 | tf_op jit(solution)/shard_map/all_to_all | solution.py:96
  41.7 0.7 reshape.54
  42.5 0.3 fusion.2
  42.8 1.6 %reshape.61 = bf16[64,4,32,32]{3,2,1,0:T(8,128)(2,1)S(1)} reshape(bf16[256,1024]{1,0:T(8,128)(2,1)S(1)} %fusion.2) | data formatting | bytes 1048576 | tf_op jit(solution)/shard_map/reshape | solution.py:42
  44.4 1.3 %fusion.11 = (bf16[96,4,32]{0,2,1:T(8,128)(2,1)S(1)}, f32[96,4,32]{0,2,1:T(8,128)}) fusion(bf16[96,64,32,1]{0,2,3,1:T(8,128)(2,1)S(1)} %bitcast.49, bf16[64,4,32,32]{3,2,1,0:T(8,128)(2,1)S(1)} %reshape.61), kind=kOutput, calls=%fused_computation.21 | convolution fusion | flops 50343936 | bytes 991232 | tf_op jit(solution)/shard_map/ijcd,sic->sjd/dot_general | solution.py:92
  45.7 22.7 %all_gather.6 = bf16[96,2048]{1,0:T(8,128)(2,1)S(1)} all-gather(bf16[96,128]{1,0:T(8,128)(2,1)S(1)} %copy-done.1), channel_id=1, replica_groups=mesh['group'=2,'col'=16] {'col'}, dimensions={1}, use_global_device_ids=true | all-gather | bytes 417792 | tf_op jit(solution)/shard_map/all_gather | solution.py:52
  68.4 0.3 copy.29
  68.8 0.9 %copy.36 = bf16[4,16,512]{2,1,0:T(8,128)(2,1)S(1)} copy(bf16[4,16,512]{2,0,1:T(4,128)(2,1)} %bitcast.8) | data formatting | bytes 131072 | tf_op jit(solution)/shard_map/all_to_all | solution.py:96
  69.7 0.3 fusion.1
  70.0 1.6 %reshape.71 = bf16[4,64,32,32]{3,2,1,0:T(8,128)(2,1)S(1)} reshape(bf16[256,1024]{1,0:T(8,128)(2,1)S(1)} %fusion.1) | data formatting | bytes 1048576 | tf_op jit(solution)/shard_map/reshape | solution.py:42
  71.6 1.3 %fusion.10 = (bf16[96,4,32]{0,2,1:T(8,128)(2,1)S(1)}, f32[96,4,32]{0,2,1:T(8,128)}) fusion(bf16[96,64,32,1]{0,2,1,3:T(8,128)(2,1)S(1)} %bitcast.50, bf16[4,64,32,32]{3,2,1,0:T(8,128)(2,1)S(1)} %reshape.71), kind=kOutput, calls=%fused_computation.20 | convolution fusion | flops 50343936 | bytes 991232 | tf_op jit(solution)/shard_map/ijcd,sjd->sic/dot_general | solution.py:110
  73.1 0.2 fusion.12
  73.3 0.2 fusion.3
  73.5 0.7 reshape.64
  (18 shorter events, 0.9 us)
Async XLA Ops:
  0.6 36.0 %copy-start = (bf16[1024,128]{1,0:T(8,128)(2,1)S(1)}, bf16[1024,128]{1,0:T(8,128)(2,1)}, u32[]{:S(2)}) copy-start(bf16[1024,128]{1,0:T(8,128)(2,1)} %param.9) | copy-start | bytes 786436
  0.6 26.7 %copy-start.3 = (bf16[256,32]{0,1:T(8,128)(2,1)S(1)}, bf16[256,32]{0,1:T(8,128)(2,1)}, u32[]{:S(2)}) copy-start(bf16[256,32]{0,1:T(8,128)(2,1)} %param.8) | copy-start | bytes 49156
  33.5 3.1 %copy-start.4 = (f32[128]{0:T(128)S(1)}, f32[128]{0:T(128)}, u32[]{:S(2)}) copy-start(f32[128]{0:T(128)} %param.10) | copy-start | bytes 1540
  37.6 31.2 %all-to-all-start = ((bf16[16,4,512]{2,1,0:T(4,128)(2,1)}), bf16[16,4,512]{2,1,0:T(4,128)(2,1)}, u32[]{:S(2)}, u32[]{:S(2)}) async-start(bf16[16,4,512]{2,1,0:T(4,128)(2,1)} %all_to_all.12), calls=%async_computation | async-start | bytes 131072 | tf_op jit(solution)/shard_map/all_to_all | solution.py:96
  42.8 3.0 %copy-start.1 = (bf16[96,128]{1,0:T(8,128)(2,1)S(1)}, bf16[96,128]{1,0:T(8,128)(2,1)}, u32[]{:S(2)}) copy-start(bf16[96,128]{1,0:T(8,128)(2,1)} %reshape.54) | copy-start | bytes 73732
  70.0 3.1 %copy-start.2 = (bf16[256,32]{0,1:T(8,128)(2,1)S(1)}, bf16[256,32]{0,1:T(8,128)(2,1)}, u32[]{:S(2)}) copy-start(bf16[256,32]{0,1:T(8,128)(2,1)} %param.7) | copy-start | bytes 49156
where the time goes:
time: 74.6 us; the launch traced here: 74.2 us
  blocking collectives  46.9 us (63%)
  local copies, waits for them, and re-layouts  14.9 us (20%)
  matrix products  6.57 us (9%)
  starting transfers between devices  4.16 us (6%)
  other arithmetic  0.87 us (1%)
  between operations  0.86 us (1%)
    all_gather x1, blocking collectives, per_device(): left_segment = lax.all_gather(first_operand_rows, 'col', axis=1, tiled=True)  24.2 us
    all_gather x1, blocking collectives, per_device(): lax.all_gather(second_operand_rows, 'col', axis=1, tiled=True)  22.7 us
    convert_element_type x1, local copies, waits for them, and re-layouts, per_device(): products.astype(jnp.bfloat16)  4.19 us
    all_to_all x1, starting transfers between devices, per_device(): lax.all_to_all(stored, 'col', split_axis=0, concat_axis=1, tiled=True)  4.16 us
    reshape x2, local copies, waits for them, and re-layouts, outer_slopes(): backward.astype(jnp.bfloat16)  3.16 us
    reshape x1, local copies, waits for them, and re-layouts, per_device(): products.astype(jnp.bfloat16)  2.23 us
    dot_general x1, matrix products, per_device(): jnp.einsum('sic,sjd->ijcd', left_block, second_operand_local, preferred_e...  1.63 us
    all_to_all x2, local copies, waits for them, and re-layouts, per_device(): lax.all_to_all(stored, 'col', split_axis=0, concat_axis=1, tiled=True)  1.52 us
  transfers between devices with their start and end apart: 1, of which 0 were waited for; matrix products, arithmetic and copies ran while one was open for 6% of the time, Pallas kernels for 0%

commit v1 on v0

--- a/solution.py
+++ b/solution.py
@@ -93,7 +93,10 @@
             "ijcd,sic->sjd", accumulate_slopes, left_block, preferred_element_type=jnp.float32
         )
     second_operand_gradient, stored, right_whole = (second_operand_gradient, stored, right_whole)
-    received = lax.all_to_all(stored, "col", split_axis=0, concat_axis=1, tiled=True)
+    received = jnp.concatenate(
+        lax.all_to_all(jnp.stack(jnp.split(stored, lax.axis_size("col"), axis=0)), "col", 0, 0),
+        axis=1,
+    )
     right_all = right_whole.reshape(alignment_row_count, residue_total_count, operand_channel_width)
     col_span = local_residue_start * max(
         max(1, 96 // local_residue_start), lax.axis_size("col") // 8

time: 74.6 us -> 83.7 us (1.12)
  local copies, waits for them, and re-layouts: 14.9 us -> 23.9 us
    unnamed x10 -> x25, local copies, waits for them, and re-layouts: 0.03 us -> 8.98 us
    all_to_all x2 -> x0, local copies, waits for them, and re-layouts: 1.52 us -> none  [per_device(): lax.all_to_all(stored, 'col', split_axis=0, concat_axis=1, tiled=True)]
  transfers between devices with their start and end apart: 1 -> 1, of which waited for: 0 -> 0; matrix products, arithmetic and copies ran while one was open for 6% -> 5% of each run, Pallas kernels for 0% -> 0%
where the time goes in v1:
time: 83.7 us; the launch traced here: 83.3 us
  blocking collectives  46.9 us (56%)
  local copies, waits for them, and re-layouts  23.9 us (29%)
  matrix products  6.59 us (8%)
  starting transfers between devices  4.15 us (5%)
  between operations  0.89 us (1%)
  other arithmetic  0.87 us (1%)
    all_gather x1, blocking collectives, per_device(): left_segment = lax.all_gather(first_operand_rows, 'col', axis=1, tiled=True)  24.2 us
    all_gather x1, blocking collectives, per_device(): lax.all_gather(second_operand_rows, 'col', axis=1, tiled=True)  22.7 us
    unnamed x25, local copies, waits for them, and re-layouts  8.98 us
    convert_element_type x1, local copies, waits for them, and re-layouts, per_device(): products.astype(jnp.bfloat16)  4.19 us
    all_to_all x1, starting transfers between devices, per_device(): lax.all_to_all(jnp.stack(jnp.split(stored, lax.axis_size('col'), axis=0))...  4.15 us
    reshape x2, local copies, waits for them, and re-layouts, outer_slopes(): backward.astype(jnp.bfloat16)  3.16 us
    reshape x1, local copies, waits for them, and re-layouts, per_device(): products.astype(jnp.bfloat16)  2.23 us
  transfers between devices with their start and end apart: 1, of which 0 were waited for; matrix products, arithmetic and copies ran while one was open for 5% of the time, Pallas kernels for 0%

profile of v1, /device:TPU:0, one launch (start us, length us, event | category | flops | bytes accessed | tf_op | source)
XLA Modules:
  0.0 83.3 jit_solution(5390616384504252940)
XLA Ops:
  0.7 1.0 %reshape.80 = bf16[384,256]{1,0:T(8,128)(2,1)S(1)} reshape(bf16[96,4,256]{2,1,0:T(4,128)(2,1)} %param.6) | data formatting | bytes 393216 | tf_op jit(solution)/shard_map/reshape | solution.py:21
  1.7 0.9 %convolution_convert_fusion = bf16[384,32]{0,1:T(8,128)(2,1)S(1)} fusion(bf16[384,256]{1,0:T(8,128)(2,1)S(1)} %reshape.80, bf16[256,32]{0,1:T(8,128)(2,1)} %param.7), kind=kOutput, calls=%fused_computation.14 | convolution fusion | flops 6303744 | bytes 237568 | tf_op jit(solution)/shard_map/dot_general | solution.py:25
  2.8 24.2 %all_gather.7 = bf16[96,2048]{1,0:T(8,128)(2,1)S(1)} all-gather(bf16[96,128]{1,0:T(8,128)(2,1)S(1)} %reshape.83), channel_id=1, replica_groups=mesh['group'=2,'col'=16] {'col'}, dimensions={1}, use_global_device_ids=true | all-gather | bytes 417792 | tf_op jit(solution)/shard_map/all_gather | solution.py:51
  27.6 1.6 %fusion = bf16[64,4,32,32]{0,3,2,1:T(8,128)(2,1)} fusion(bf16[96,64,32]{0,2,1:T(8,128)(2,1)S(1)} %bitcast.48, bf16[96,4,32,1]{2,1,0,3:T(4,128)(2,1)S(1)} %bitcast.51), kind=kOutput, calls=%fused_computation.1 | convolution fusion | flops 50855936 | bytes 942080 | tf_op jit(solution)/shard_map/sic,sjd->ijcd/dot_general | solution.py:68
  29.3 4.2 %copy.50 = bf16[64,4,32,32]{3,2,1,0:T(8,128)(2,1)S(1)} copy(bf16[64,4,32,32]{0,3,2,1:T(8,128)(2,1)} %fusion) | data formatting | bytes 1048576 | tf_op jit(solution)/shard_map/convert_element_type | solution.py:76
  33.5 2.2 %reshape.85 = bf16[256,1024]{1,0:T(8,128)(2,1)S(1)} reshape(bf16[64,4,32,32]{3,2,1,0:T(8,128)(2,1)S(1)} %copy.50) | data formatting | bytes 1048576 | tf_op jit(solution)/shard_map/reshape | solution.py:76
  35.7 0.9 %convert_multiply_fusion = f32[64,4,128]{2,1,0:T(4,128)S(1)} fusion(bf16[64,4,128]{2,1,0:T(4,128)(2,1)} %param.11), kind=kLoop, calls=%fused_computation.18 | loop fusion | flops 65536 | bytes 196608 | tf_op jit(solution)/shard_map/mul | solution.py:84
  36.9 0.6 constant_dynamic-update-slice_fusion.15
  37.7 0.6 constant_dynamic-update-slice_fusion.14
  38.9 0.6 constant_dynamic-update-slice_fusion.12
  39.5 0.6 constant_dynamic-update-slice_fusion.11
  41.3 0.6 constant_dynamic-update-slice_fusion.8
  41.9 0.6 constant_dynamic-update-slice_fusion.7
  42.5 0.6 constant_dynamic-update-slice_fusion.6
  44.3 0.6 constant_dynamic-update-slice_fusion.3
  46.7 4.2 %all-to-all-start = ((bf16[16,4,512]{2,1,0:T(4,128)(2,1)}), bf16[16,4,512]{2,1,0:T(4,128)(2,1)}, u32[]{:S(2)}, u32[]{:S(2)}) async-start(bf16[16,4,512]{2,1,0:T(4,128)(2,1)} %constant_dynamic-update-slice_fusion), calls=%async_computation | async-start | bytes 131072 | tf_op jit(solution)/shard_map/all_to_all | solution.py:97
  50.8 0.7 reshape.81
  51.9 1.6 %reshape.88 = bf16[64,4,32,32]{3,2,1,0:T(8,128)(2,1)S(1)} reshape(bf16[256,1024]{1,0:T(8,128)(2,1)S(1)} %fusion.2) | data formatting | bytes 1048576 | tf_op jit(solution)/shard_map/reshape | solution.py:42
  53.4 1.3 %fusion.12 = (bf16[96,4,32]{0,2,1:T(8,128)(2,1)S(1)}, f32[96,4,32]{0,2,1:T(8,128)}) fusion(bf16[96,64,32,1]{0,2,3,1:T(8,128)(2,1)S(1)} %bitcast.49, bf16[64,4,32,32]{3,2,1,0:T(8,128)(2,1)S(1)} %reshape.88), kind=kOutput, calls=%fused_computation.38 | convolution fusion | flops 50343936 | bytes 991232 | tf_op jit(solution)/shard_map/ijcd,sic->sjd/dot_general | solution.py:92
  54.8 22.7 %all_gather.6 = bf16[96,2048]{1,0:T(8,128)(2,1)S(1)} all-gather(bf16[96,128]{1,0:T(8,128)(2,1)S(1)} %copy-done.1), channel_id=1, replica_groups=mesh['group'=2,'col'=16] {'col'}, dimensions={1}, use_global_device_ids=true | all-gather | bytes 417792 | tf_op jit(solution)/shard_map/all_gather | solution.py:52
  77.9 0.9 %copy.51 = bf16[4,16,512]{2,1,0:T(8,128)(2,1)S(1)} copy(bf16[4,16,512]{2,0,1:T(4,128)(2,1)} %bitcast.8) | data formatting | bytes 131072 | tf_op jit(solution)/shard_map/reshape | solution.py:96
  79.1 1.6 %reshape.98 = bf16[4,64,32,32]{3,2,1,0:T(8,128)(2,1)S(1)} reshape(bf16[256,1024]{1,0:T(8,128)(2,1)S(1)} %fusion.1) | data formatting | bytes 1048576 | tf_op jit(solution)/shard_map/reshape | solution.py:42
  80.7 1.3 %fusion.11 = (bf16[96,4,32]{0,2,1:T(8,128)(2,1)S(1)}, f32[96,4,32]{0,2,1:T(8,128)}) fusion(bf16[96,64,32,1]{0,2,1,3:T(8,128)(2,1)S(1)} %bitcast.50, bf16[4,64,32,32]{3,2,1,0:T(8,128)(2,1)S(1)} %reshape.98), kind=kOutput, calls=%fused_computation.37 | convolution fusion | flops 50343936 | bytes 991232 | tf_op jit(solution)/shard_map/ijcd,sjd->sic/dot_general | solution.py:113
  82.6 0.7 reshape.91
  (50 shorter events, 7.6 us)
Async XLA Ops:
  0.6 36.0 %copy-start = (bf16[1024,128]{1,0:T(8,128)(2,1)S(1)}, bf16[1024,128]{1,0:T(8,128)(2,1)}, u32[]{:S(2)}) copy-start(bf16[1024,128]{1,0:T(8,128)(2,1)} %param.9) | copy-start | bytes 786436
  0.6 26.7 %copy-start.3 = (bf16[256,32]{0,1:T(8,128)(2,1)S(1)}, bf16[256,32]{0,1:T(8,128)(2,1)}, u32[]{:S(2)}) copy-start(bf16[256,32]{0,1:T(8,128)(2,1)} %param.8) | copy-start | bytes 49156
  33.5 3.1 %copy-start.4 = (f32[128]{0:T(128)S(1)}, f32[128]{0:T(128)}, u32[]{:S(2)}) copy-start(f32[128]{0:T(128)} %param.10) | copy-start | bytes 1540
  46.7 31.2 %all-to-all-start = ((bf16[16,4,512]{2,1,0:T(4,128)(2,1)}), bf16[16,4,512]{2,1,0:T(4,128)(2,1)}, u32[]{:S(2)}, u32[]{:S(2)}) async-start(bf16[16,4,512]{2,1,0:T(4,128)(2,1)} %constant_dynamic-update-slice_fusion), calls=%async_computation | async-start | bytes 131072 | tf_op jit(solution)/shard_map/all_to_all | solution.py:97
  51.8 3.0 %copy-start.1 = (bf16[96,128]{1,0:T(8,128)(2,1)S(1)}, bf16[96,128]{1,0:T(8,128)(2,1)}, u32[]{:S(2)}) copy-start(bf16[96,128]{1,0:T(8,128)(2,1)} %reshape.81) | copy-start | bytes 73732
  79.1 3.1 %copy-start.2 = (bf16[256,32]{0,1:T(8,128)(2,1)S(1)}, bf16[256,32]{0,1:T(8,128)(2,1)}, u32[]{:S(2)}) copy-start(bf16[256,32]{0,1:T(8,128)(2,1)} %param.7) | copy-start | bytes 49156
